TPU v7x, 32 devices: a whole 2x2x4 slice. The times are simulated.
32 devices in a mesh: ctx: 16 (over z, y, x), head: 2 (over core).
Axes of the slice: x: 2, y: 2, z: 4, core: 2. Of those that a mesh axis runs over, the one named last changes fastest.
Arguments:
- queries: float32 [8192, 512], P('ctx', 'head'), may hold values from -1024 to 1024
- keys: float32 [8192, 128], P('ctx'), may hold values from -1024 to 1024
- values: float32 [8192, 128], P('ctx'), may hold values from -6 to 6
- cotangent: float32 [8192, 512], P('ctx', 'head'), may hold values from -384 to 384
- source_ids: int32 [8192], P('ctx'), may hold values from 0 to 63
- source_weights: float32 [64], replicated, may hold values from 0.25 to 4
- q_feature: float32 [4, 128, 128], P('head'), may hold values from -4 to 4
- k_feature: float32 [128, 128], replicated, may hold values from -4 to 4
Outputs:
- grad_queries: float32 [8192, 512], P('ctx', 'head')
- grad_keys: float32 [8192, 128], P(('ctx', 'head'))
- grad_values: float32 [8192, 128], P(('ctx', 'head'))
- grad_q_feature: float32 [4, 128, 128], P('head')
- grad_k_feature: float32 [128, 128], replicated
All inputs are finite; a program needn't handle non-finite values.
Results may differ from a plain program's by a relative error of at most 0.0015.
Values sent between devices are 32-bit elements; how exact they have to be, the bound alone decides.
No kernel may reach another device: no remote copies, remote signals or barrier semaphores. Data moves between devices by JAX's collectives and lax.ppermute only.
A program may use at most 64 MiB of HBM per device.

v0:
```python
import jax
import jax.numpy as jnp
from jax import lax
from jax.sharding import PartitionSpec as P


def entering(value, axis, join, neutral, backward):
    count, mine = (lax.axis_size(axis), lax.axis_index(axis))
    pieces = jax.tree.map(lambda part: lax.all_gather(part, axis), value)
    if backward:
        pieces = jax.tree.map(lambda part: part[::-1], pieces)
        mine = count - 1 - mine
    total = jax.tree.map(
        lambda part, zero: jnp.full_like(part, 0) + jnp.asarray(zero, part.dtype), value, neutral
    )

    def turn(position, total):
        longer = join(total, jax.tree.map(lambda part: part[position], pieces))
        return jax.tree.map(lambda new, old: jnp.where(position < mine, new, old), longer, total)

    return lax.fori_loop(0, count - 1, turn, total)


def matmul(left, right):
    return jnp.dot(left, right, precision=lax.Precision.HIGHEST, preferred_element_type=jnp.float32)


def product(form, left, right):
    return jnp.einsum(
        form, left, right, precision=lax.Precision.HIGHEST, preferred_element_type=jnp.float32
    )


def feature_map(inputs, weight):
    logits = matmul(inputs, weight)
    upper = jax.nn.softmax(logits, axis=-1)
    lower = jax.nn.softmax(-logits, axis=-1)
    return (jnp.concatenate([upper, lower], axis=-1), upper, lower)


def feature_back(inputs, weight, upper, lower, grad_feat):
    half = upper.shape[-1]
    grad_upper = grad_feat[:, :half]
    grad_lower = grad_feat[:, half:]
    grad_logits = upper * (grad_upper - jnp.sum(upper * grad_upper, axis=-1, keepdims=True))
    grad_logits = grad_logits - lower * (
        grad_lower - jnp.sum(lower * grad_lower, axis=-1, keepdims=True)
    )
    return (matmul(grad_logits, weight.T), matmul(inputs.T, grad_logits))


def causal_mask(count):
    row_index = lax.broadcasted_iota(jnp.int32, (count, count), 0)
    col_index = lax.broadcasted_iota(jnp.int32, (count, count), 1)
    return (row_index >= col_index).astype(jnp.float32)


def add_pair(earlier, later):
    return (earlier[0] + later[0], earlier[1] + later[1])


def block_terms(query_c, key_c, value_c, scaled_c, prefix, prefix_tot):
    lower_mask = causal_mask(query_c.shape[1])
    scores = product("ncf,ndf->ncd", query_c, key_c) * lower_mask
    numerator = product("ncd,nde->nce", scores, value_c) + product("ncf,nfe->nce", query_c, prefix)
    normalizer = jnp.sum(scores, axis=2) + product("ncf,nf->nc", query_c, prefix_tot)
    output = numerator / normalizer[..., None]
    grad_numer = scaled_c / normalizer[..., None]
    grad_norm = -jnp.sum(scaled_c * output, axis=2) / normalizer
    grad_scores = (product("nce,nde->ncd", grad_numer, value_c) + grad_norm[..., None]) * lower_mask
    grad_query = (
        product("ncd,ndf->ncf", grad_scores, key_c)
        + product("nce,nfe->ncf", grad_numer, prefix)
        + grad_norm[..., None] * prefix_tot[:, None, :]
    )
    grad_key = product("ncd,ncf->ndf", grad_scores, query_c)
    grad_value = product("ncd,nce->nde", scores, grad_numer)
    carried = product("ncf,nce->nfe", query_c, grad_numer)
    carried_totals = product("nc,ncf->nf", grad_norm, query_c)
    return (grad_query, grad_key, grad_value, carried, carried_totals)


def on_device(queries, keys, values, cotangent, source_ids, source_weights, q_feature, k_feature):
    head_count = q_feature.shape[0]
    width = q_feature.shape[1]
    features = 2 * q_feature.shape[2]
    rows = queries.shape[0]
    piece = min(128, rows)
    pieces = rows // piece
    source_index = lax.broadcasted_iota(jnp.int32, (1, source_weights.shape[0]), 1)
    lookup = (source_ids[:, None] == source_index).astype(jnp.float32)
    weight = jnp.sum(lookup * source_weights[None, :], axis=1)
    key_feat, key_upper, key_lower = feature_map(keys, k_feature)
    key_c = key_feat.reshape(pieces, piece, features)
    value_c = values.reshape(pieces, piece, width)
    piece_state = product("ncf,nce->nfe", key_c, value_c)
    piece_tot = jnp.sum(key_c, axis=1)
    share = features // lax.axis_size("head")
    offset = lax.axis_index("head") * share
    slab_feat = lax.dynamic_slice_in_dim(key_feat, offset, share, 1)
    slab_local = (
        lax.dynamic_slice_in_dim(jnp.sum(piece_state, axis=0), offset, share, 0),
        lax.dynamic_slice_in_dim(jnp.sum(piece_tot, axis=0), offset, share, 0),
    )
    slab_zero = (jnp.zeros((share, width), jnp.float32), jnp.zeros((share,), jnp.float32))
    slab_before = entering(slab_local, "ctx", add_pair, slab_zero, False)
    earlier, earlier_totals = (
        lax.all_gather(slab_before[0], "head", axis=0, tiled=True),
        lax.all_gather(slab_before[1], "head", axis=0, tiled=True),
    )
    prefix = jnp.cumsum(piece_state, axis=0) - piece_state + earlier[None]
    prefix_tot = jnp.cumsum(piece_tot, axis=0) - piece_tot + earlier_totals[None]
    grad_keyfeat = jnp.zeros(key_feat.shape, jnp.float32)
    grad_vals = jnp.zeros(values.shape, jnp.float32)
    piece_carried = jnp.zeros((pieces, features, width), jnp.float32)
    piece_carried_tot = jnp.zeros((pieces, features), jnp.float32)
    query_grads = []
    weight_grads = []
    for head in range(head_count):
        query_head = queries[:, head * width : (head + 1) * width]
        query_feat, query_upper, query_lower = feature_map(query_head, q_feature[head])
        scaled = cotangent[:, head * width : (head + 1) * width] * weight[:, None]
        grad_query, grad_key, grad_value, carried, carried_totals = block_terms(
            query_feat.reshape(pieces, piece, features),
            key_c,
            value_c,
            scaled.reshape(pieces, piece, width),
            prefix,
            prefix_tot,
        )
        grad_head, grad_weight = feature_back(
            query_head,
            q_feature[head],
            query_upper,
            query_lower,
            grad_query.reshape(rows, features),
        )
        query_grads.append(grad_head)
        weight_grads.append(grad_weight)
        grad_keyfeat = grad_keyfeat + grad_key.reshape(rows, features)
        grad_vals = grad_vals + grad_value.reshape(rows, width)
        piece_carried = piece_carried + carried
        piece_carried_tot = piece_carried_tot + carried_totals
    carried_all = jnp.sum(piece_carried, axis=0)
    carried_tot = jnp.sum(piece_carried_tot, axis=0)
    inner_later = carried_all[None] - jnp.cumsum(piece_carried, axis=0)
    inner_tot = carried_tot[None] - jnp.cumsum(piece_carried_tot, axis=0)
    grad_keyfeat = grad_keyfeat + (
        product("nce,nfe->ncf", value_c, inner_later) + inner_tot[:, None, :]
    ).reshape(rows, features)
    grad_vals = grad_vals + product("ncf,nfe->nce", key_c, inner_later).reshape(rows, width)
    folded, folded_tot = (
        lax.psum_scatter(carried_all, "head", scatter_dimension=0, tiled=True),
        lax.psum_scatter(carried_tot, "head", scatter_dimension=0, tiled=True),
    )
    later, later_tot = entering((folded, folded_tot), "ctx", add_pair, slab_zero, True)
    slab_grad = matmul(values, later.T) + later_tot[None, :]
    current = lax.dynamic_slice_in_dim(grad_keyfeat, offset, share, 1)
    grad_keyfeat = lax.dynamic_update_slice_in_dim(grad_keyfeat, current + slab_grad, offset, 1)
    grad_vals = grad_vals + matmul(slab_feat, later)
    grad_key_part, grad_kweight = feature_back(keys, k_feature, key_upper, key_lower, grad_keyfeat)
    grad_keys, grad_values = (
        lax.psum_scatter(grad_key_part, "head", scatter_dimension=0, tiled=True),
        lax.psum_scatter(grad_vals, "head", scatter_dimension=0, tiled=True),
    )
    grad_qweight = lax.psum(jnp.stack(weight_grads, axis=0), "ctx")
    grad_kweight = lax.psum(grad_kweight, ("ctx", "head"))
    return (
        jnp.concatenate(query_grads, axis=1),
        grad_keys,
        grad_values,
        grad_qweight,
        grad_kweight,
    )


def solution(mesh):
    placed = (
        P("ctx", "head"),
        P("ctx", None),
        P("ctx", None),
        P("ctx", "head"),
        P("ctx"),
        P(),
        P("head", None, None),
        P(),
    )
    return jax.shard_map(
        on_device,
        mesh=mesh,
        in_specs=placed,
        out_specs=(
            P("ctx", "head"),
            P(("ctx", "head"), None),
            P(("ctx", "head"), None),
            P("head", None, None),
            P(),
        ),
        check_vma=False,
    )
```

profile of v0, /device:TPU:0, one launch (start us, length us, event | category | flops | bytes accessed | tf_op | source)
XLA Modules:
  0.0 441.5 jit_solution(6858536777643410984)
XLA Ops:
  7.2 1.4 fusion.102
  16.1 42.4 %all-gather.4 = f32[16,1,128]{2,1,0:T(1,128)S(1)} all-gather(f32[1,1,128]{2,1,0:T(1,128)S(1)} %dynamic-slice_bitcast_fusion.1), channel_id=3, replica_groups=mesh['ctx'=16,'head'=2] {'ctx'}, dimensions={0}, use_global_device_ids=true | all-gather | bytes 8704 | tf_op jit(solution)/shard_map/all_gather | solution.py:9
  59.9 1.8 fusion.107
  61.7 1.8 fusion.109
  63.4 5.7 %all-gather.10.cloned.1.call-done = f32[2048,128]{1,0:T(8,128)} async-done(((f32[128,128]{1,0:T(8,128)}), f32[2048,128]{1,0:T(8,128)}) %all-gather.10.cloned.1.call-update) | async-done | bytes 1048592 | tf_op jit(solution)/shard_map/all_gather | solution.py:9
  69.2 13.6 %while.32 = (s32[]{:T(128)}, f32[128,128]{1,0:T(8,128)S(1)}, f32[128]{0:T(128)S(1)}, s32[]{:T(128)}, f32[16,128,128]{2,1,0:T(8,128)}, /*index=5*/f32[16,128]{1,0:T(8,128)S(1)}, s32[]{:T(128)}, s32[]{:T(128)}) while((s32[]{:T(128)}, f32[128,128]{1,0:T(8,128)S(1)}, f32[128]{0:T(128)S(1)}, s32[]{:T(128)}, ...), condition=%wide.region_15.16_spmd.clone, body=%wide.region_14.15_spmd.clone.sunk | while | flops 49540 | bytes 198267 | solution.py:21
  69.2 0.9 add_select_fusion.4
  70.1 0.9 add_select_fusion.4
  71.0 0.9 add_select_fusion.4
  71.9 0.9 add_select_fusion.4
  72.8 0.9 add_select_fusion.4
  73.7 0.9 add_select_fusion.4
  82.8 1.8 all-gather.5
  84.8 1.0 fusion.22
  85.8 1.0 fusion.42
  86.8 2.1 all_gather.35
  88.9 1.1 fusion.20
  90.0 1.1 fusion.40
  93.0 1.4 fusion.45
  94.4 1.4 fusion.33
  95.9 1.4 fusion.36
  100.2 2.5 all-reduce
  103.7 1.4 convolution_add_fusion.2
  108.9 2.1 fusion.110
  111.1 1.2 reduce-window_subtract_fusion
  112.3 1.4 fusion.2
  113.7 3.9 reduce-scatter.4.cloned.1.call-done
  117.8 41.0 %all-gather.6 = f32[16,1,128]{2,1,0:T(1,128)S(1)} all-gather(f32[1,1,128]{2,1,0:T(1,128)S(1)} %dynamic-slice_bitcast_fusion), channel_id=5, replica_groups=mesh['ctx'=16,'head'=2] {'ctx'}, dimensions={0}, use_global_device_ids=true | all-gather | bytes 8704 | tf_op jit(solution)/shard_map/all_gather | solution.py:9
  158.8 1.8 copy.212
  162.5 1.2 copy.209
  163.7 1.8 copy.211
  165.5 1.2 multiply_reduce_fusion.2
  166.8 0.9 copy-done.13
  171.2 1.0 fusion.28
  173.0 3.7 all-gather.12.cloned.1.call-done
  176.7 1.3 rev.6
  178.0 1.0 while.33
  180.5 1.0 convolution_bitcast_fusion
  181.6 1.3 convolution_add_fusion.5
  183.7 1.3 fusion.111
  185.0 0.9 copy-done.4
  186.8 1.0 copy.180
  187.8 99.0 %all-reduce.4.cloned.1.call-done = f32[2,128,128]{1,2,0:T(8,128)} async-done(((f32[2,128,128]{1,2,0:T(8,128)}), f32[2,128,128]{1,2,0:T(8,128)}) %all-reduce.4.cloned.1.call-update) | async-done | bytes 131088 | tf_op jit(solution)/shard_map/psum | solution.py:166
  286.8 1.7 copy.181
  288.4 122.9 %all-reduce.6.cloned.1.call-done = f32[128,128]{0,1:T(8,128)} async-done(((f32[128,128]{0,1:T(8,128)}), f32[128,128]{0,1:T(8,128)}) %all-reduce.6.cloned.1.call-update) | async-done | bytes 65552 | tf_op jit(solution)/shard_map/psum | solution.py:167
  411.3 1.6 copy.182
  412.8 10.1 %reduce-scatter.8.cloned.1.call-done = f32[256,128]{1,0:T(8,128)} async-done(((f32[512,128]{1,0:T(8,128)}), f32[256,128]{1,0:T(8,128)}) %reduce-scatter.8.cloned.1.call-update) | async-done | bytes 131088 | tf_op jit(solution)/shard_map/reduce_scatter | solution.py:164
  422.9 11.7 %reduce-scatter.6.cloned.1.call-done = f32[256,128]{1,0:T(8,128)} async-done(((f32[512,128]{1,0:T(8,128)}), f32[256,128]{1,0:T(8,128)}) %reduce-scatter.6.cloned.1.call-update) | async-done | bytes 131088 | tf_op jit(solution)/shard_map/reduce_scatter | solution.py:163
  (213 shorter events, 35.9 us)
Async XLA Ops:
  7.2 1.8 copy-start
  7.2 62.0 %all-gather.10.cloned.1.call-start = ((), (), s32[]{:S(2)}) async-start(), calls=%async_computation.8 | async-start | bytes 1114112 | tf_op jit(solution)/shard_map/all_gather | solution.py:9
  9.0 2.0 copy-start.29
  10.3 0.7 copy-start.38
  10.3 0.7 copy-start.39
  10.3 107.3 %reduce-scatter.4.cloned.1.call-start = ((), (), s32[]{:S(2)}) async-start(), calls=%async_computation.3 | async-start | bytes 196608 | tf_op jit(solution)/shard_map/reduce_scatter | solution.py:153
  13.1 45.4 %copy-start.12 = (f32[512,256]{1,0:T(8,128)S(1)}, f32[512,256]{1,0:T(8,128)}, u32[]{:S(2)}) copy-start(f32[512,256]{1,0:T(8,128)} %param.12) | copy-start | bytes 1572868
  13.5 0.7 copy-start.14
  13.5 45.1 %copy-start.27 = (f32[2,128,128]{2,1,0:T(8,128)S(1)}, f32[2,128,128]{2,1,0:T(8,128)}, u32[]{:S(2)}) copy-start(f32[2,128,128]{2,1,0:T(8,128)} %param.18) | copy-start | bytes 393220
  14.2 0.7 copy-start.40
  58.6 3.1 copy-start.24
  69.2 15.4 %copy-start.15 = (f32[4,256]{0,1:T(8,128)S(1)}, f32[4,256]{0,1:T(8,128)}, u32[]{:S(2)}) copy-start(f32[4,256]{0,1:T(8,128)} %copy-done.14) | copy-start | bytes 12292
  90.0 1.8 copy-start.16
  90.0 1.8 copy-start.31
  91.1 0.7 copy-start.37
  91.8 4.1 copy-start.33
  91.8 0.8 copy-start.25
  95.9 2.1 copy-start.1
  95.9 2.1 copy-start.20
  97.3 0.7 copy-start.36
  102.6 1.0 copy-start.11
  105.7 1.2 copy-start.10
  105.7 1.3 copy-start.17
  105.7 1.3 copy-start.34
  107.7 1.2 copy-start.26
  111.0 65.7 %all-gather.12.cloned.1.call-start = ((), (), s32[]{:S(2)}) async-start(), calls=%async_computation.9 | async-start | bytes 1114112 | tf_op jit(solution)/shard_map/all_gather | solution.py:9
  111.1 1.2 copy-start.9
  117.6 169.1 %all-reduce.4.cloned.1.call-start = ((), (), s32[]{:S(2)}) async-start(), calls=%async_computation.6 | async-start | bytes 262144 | tf_op jit(solution)/shard_map/psum | solution.py:166
  158.8 1.9 copy-start.22
  160.6 1.0 copy-start.23
  165.5 1.2 copy-start.7
  165.5 1.2 copy-start.8
  166.7 1.0 copy-start.13
  167.7 0.7 copy-start.3
  167.7 1.0 copy-start.5
  167.7 1.1 copy-start.6
  169.1 1.1 copy-start.32
  169.5 1.0 copy-start.18
  171.2 1.1 copy-start.2
  171.2 1.1 copy-start.21
  173.0 238.3 %all-reduce.6.cloned.1.call-start = ((), (), s32[]{:S(2)}) async-start(), calls=%async_computation.7 | async-start | bytes 131072 | tf_op jit(solution)/shard_map/psum | solution.py:167
  176.7 1.3 copy-start.35
  179.5 1.0 copy-start.19
  181.5 241.4 %reduce-scatter.8.cloned.1.call-start = ((), (), s32[]{:S(2)}) async-start(), calls=%async_computation.5 | async-start | bytes 393216 | tf_op jit(solution)/shard_map/reduce_scatter | solution.py:164
  182.9 0.8 copy-start.30
  182.9 251.7 %reduce-scatter.6.cloned.1.call-start = ((), (), s32[]{:S(2)}) async-start(), calls=%async_computation.4 | async-start | bytes 393216 | tf_op jit(solution)/shard_map/reduce_scatter | solution.py:163
  183.7 1.3 copy-start.28
  185.0 0.9 copy-start.4
Sparse Core Ops, SparseCore 0:
  11.3 57.8 all-gather.9
  111.1 6.4 reduce-scatter.3
  120.4 56.2 all-gather.11
  182.6 104.1 all-reduce.3
  292.8 118.4 all-reduce.5
  413.9 8.9 reduce-scatter.7
  425.7 8.8 reduce-scatter.5
where the time goes:
time: 443 us; the launch traced here: 441 us
  waiting for transfers between devices  257 us (58%)
  blocking collectives  89.8 us (20%)
  matrix products  32.6 us (7%)
  local copies, waits for them, and re-layouts  26.5 us (6%)
  other arithmetic  19 us (4%)
  between operations  15.4 us (3%)
    psum x1, waiting for transfers between devices, on_device(): grad_kweight = lax.psum(grad_kweight, ('ctx', 'head'))  123 us
    psum x1, waiting for transfers between devices, on_device(): grad_qweight = lax.psum(jnp.stack(weight_grads, axis=0), 'ctx')  99 us
    all_gather x2, blocking collectives, entering(): pieces = jax.tree.map(lambda part: lax.all_gather(part, axis), value)  83.5 us
    dot_general x25, matrix products, product(): jnp.einsum(form, left, right, precision=lax.Precision.HIGHEST, preferred_...  24.8 us
    unnamed x92, local copies, waits for them, and re-layouts  19.6 us
    select_n x60, other arithmetic, turn(): jnp.where(position < mine, new, old)  13.7 us
    reduce_scatter x1, waiting for transfers between devices, on_device(): lax.psum_scatter(grad_key_part, 'head', scatter_dimension=0, tiled=True)  11.7 us
    reduce_scatter x1, waiting for transfers between devices, on_device(): lax.psum_scatter(grad_vals, 'head', scatter_dimension=0, tiled=True)  10.1 us
  transfers between devices with their start and end apart: 7, of which 7 were waited for; matrix products, arithmetic and copies ran while one was open for 8% of the time, Pallas kernels for 0%

commit v1 on v0

--- a/solution.py
+++ b/solution.py
@@ -164,7 +164,7 @@
         lax.psum_scatter(grad_vals, "head", scatter_dimension=0, tiled=True),
     )
     grad_qweight = lax.psum(jnp.stack(weight_grads, axis=0), "ctx")
-    grad_kweight = lax.psum(grad_kweight, ("ctx", "head"))
+    grad_kweight = jnp.sum(lax.all_gather(grad_kweight, ("ctx", "head")), axis=0)
     return (
         jnp.concatenate(query_grads, axis=1),
         grad_keys,

time: 443 us -> 399 us (0.901)
  waiting for transfers between devices: 257 us -> 204 us
  other arithmetic: 19 us -> 33.9 us
  local copies, waits for them, and re-layouts: 26.5 us -> 20.5 us
    psum x1 -> x0, waiting for transfers between devices: 123 us -> none  [on_device(): grad_kweight = lax.psum(grad_kweight, ('ctx', 'head'))]
    all_gather x0 -> x1, waiting for transfers between devices: none -> 57.2 us  [on_device(): lax.all_gather(grad_kweight, ('ctx', 'head'))]
    all_gather x2, waiting for transfers between devices: 9.41 us -> 43.8 us  [entering(): pieces = jax.tree.map(lambda part: lax.all_gather(part, axis), value)]
    psum x1, waiting for transfers between devices: 99 us -> 84.3 us  [on_device(): grad_qweight = lax.psum(jnp.stack(weight_grads, axis=0), 'ctx')]
    select_n x60, other arithmetic: 13.7 us -> 26.5 us  [turn(): jnp.where(position < mine, new, old)]
    unnamed x92 -> x81, local copies, waits for them, and re-layouts: 19.6 us -> 12.5 us
  transfers between devices with their start and end apart: 7 -> 7, of which waited for: 7 -> 6; matrix products, arithmetic and copies ran while one was open for 8% -> 14% of each run, Pallas kernels for 0% -> 0%
where the time goes in v1:
time: 399 us; the launch traced here: 397 us
  waiting for transfers between devices  204 us (51%)
  blocking collectives  87.3 us (22%)
  matrix products  34.7 us (9%)
  other arithmetic  33.9 us (8%)
  local copies, waits for them, and re-layouts  20.5 us (5%)
  between operations  15.5 us (4%)
    psum x1, waiting for transfers between devices, on_device(): grad_qweight = lax.psum(jnp.stack(weight_grads, axis=0), 'ctx')  84.3 us
    all_gather x2, blocking collectives, entering(): pieces = jax.tree.map(lambda part: lax.all_gather(part, axis), value)  80.9 us
    all_gather x1, waiting for transfers between devices, on_device(): lax.all_gather(grad_kweight, ('ctx', 'head'))  57.2 us
    all_gather x2, waiting for transfers between devices, entering(): pieces = jax.tree.map(lambda part: lax.all_gather(part, axis), value)  43.8 us
    select_n x60, other arithmetic, turn(): jnp.where(position < mine, new, old)  26.5 us
    dot_general x25, matrix products, product(): jnp.einsum(form, left, right, precision=lax.Precision.HIGHEST, preferred_...  25.1 us
    unnamed x81, local copies, waits for them, and re-layouts  12.5 us
    reduce_scatter x1, waiting for transfers between devices, on_device(): lax.psum_scatter(grad_key_part, 'head', scatter_dimension=0, tiled=True)  11.7 us
  transfers between devices with their start and end apart: 7, of which 6 were waited for; matrix products, arithmetic and copies ran while one was open for 14% of the time, Pallas kernels for 0%

profile of v1, /device:TPU:0, one launch (start us, length us, event | category | flops | bytes accessed | tf_op | source)
XLA Modules:
  0.0 396.6 jit_solution(15787334463513923808)
XLA Ops:
  7.2 1.4 fusion.102
  10.5 1.2 slice_multiply_fusion.1
  15.5 42.4 %all-gather.5 = f32[16,1,128]{2,1,0:T(1,128)S(1)} all-gather(f32[1,1,128]{2,1,0:T(1,128)S(1)} %dynamic-slice_bitcast_fusion.1), channel_id=3, replica_groups=mesh['ctx'=16,'head'=2] {'ctx'}, dimensions={0}, use_global_device_ids=true | all-gather | bytes 8704 | tf_op jit(solution)/shard_map/all_gather | solution.py:9
  58.0 1.3 fusion.103
  59.3 1.3 fusion.101
  60.9 1.8 fusion.107
  62.7 1.8 fusion.109
  64.5 4.7 %all-gather.12.cloned.1.call-done = f32[2048,128]{1,0:T(8,128)} async-done(((f32[128,128]{1,0:T(8,128)}), f32[2048,128]{1,0:T(8,128)}) %all-gather.12.cloned.1.call-update) | async-done | bytes 1048592 | tf_op jit(solution)/shard_map/all_gather | solution.py:9
  69.2 13.6 %while.32 = (s32[]{:T(128)}, f32[128,128]{1,0:T(8,128)S(1)}, f32[128]{0:T(128)S(1)}, s32[]{:T(128)}, f32[16,128,128]{2,1,0:T(8,128)}, /*index=5*/f32[16,128]{1,0:T(8,128)S(1)}, s32[]{:T(128)}, s32[]{:T(128)}) while((s32[]{:T(128)}, f32[128,128]{1,0:T(8,128)S(1)}, f32[128]{0:T(128)S(1)}, s32[]{:T(128)}, ...), condition=%wide.region_15.16_spmd.clone, body=%wide.region_14.15_spmd.clone.sunk | while | flops 49540 | bytes 198267 | solution.py:21
  82.7 1.8 all-gather.6
  84.7 1.0 fusion.22
  85.7 1.0 fusion.42
  86.8 2.1 all_gather.41
  88.9 1.1 fusion.20
  90.0 1.1 fusion.40
  92.7 1.4 fusion.36
  94.8 1.1 fusion.12
  96.5 2.5 all-reduce
  103.3 1.3 fusion.110
  104.7 38.5 %all-gather.7 = f32[16,1,128]{2,1,0:T(1,128)S(1)} all-gather(f32[1,1,128]{2,1,0:T(1,128)S(1)} %dynamic-slice_bitcast_fusion), channel_id=5, replica_groups=mesh['ctx'=16,'head'=2] {'ctx'}, dimensions={0}, use_global_device_ids=true | all-gather | bytes 8704 | tf_op jit(solution)/shard_map/all_gather | solution.py:9
  143.2 1.8 copy.210
  145.9 1.8 copy.208
  147.7 0.9 reduce-window_subtract_fusion
  148.9 1.5 fusion.45
  150.5 1.6 convolution_add_fusion.2
  152.0 1.4 fusion.2
  153.5 1.2 copy.207
  154.7 1.8 copy.209
  156.5 1.2 multiply_reduce_fusion.2
  157.7 1.1 multiply_subtract_fusion.1
  160.7 39.1 %all-gather.14.cloned.1.call-done = f32[2048,128]{1,0:T(8,128)} async-done(((f32[128,128]{1,0:T(8,128)}), f32[2048,128]{1,0:T(8,128)}) %all-gather.14.cloned.1.call-update) | async-done | bytes 1048592 | tf_op jit(solution)/shard_map/all_gather | solution.py:9
  199.8 2.4 rev.6
  202.1 13.7 %while.33 = (s32[]{:T(128)}, f32[128,128]{1,0:T(8,128)S(1)}, f32[128]{0:T(128)S(1)}, s32[]{:T(128)}, f32[16,128,128]{2,1,0:T(8,128)}, /*index=5*/f32[16,128]{1,0:T(8,128)S(1)}, s32[]{:T(128)}, s32[]{:T(128)}) while((s32[]{:T(128)}, f32[128,128]{1,0:T(8,128)S(1)}, f32[128]{0:T(128)S(1)}, s32[]{:T(128)}, ...), condition=%wide.region_35.36_spmd.clone, body=%wide.region_34.35_spmd.clone.sunk | while | flops 49540 | bytes 198267 | solution.py:21
  202.2 0.9 add_select_fusion.5
  209.5 0.9 add_select_fusion.5
  210.4 0.9 add_select_fusion.5
  216.5 1.0 convolution_bitcast_fusion
  217.6 1.6 fusion.100
  219.2 1.0 fusion.28
  221.0 1.3 convolution_add_fusion.5
  222.8 1.3 fusion.111
  224.6 1.0 copy.178
  225.6 84.3 %all-reduce.3.cloned.1.call-done = f32[2,128,128]{1,2,0:T(8,128)} async-done(((f32[2,128,128]{1,2,0:T(8,128)}), f32[2,128,128]{1,2,0:T(8,128)}) %all-reduce.3.cloned.1.call-update) | async-done | bytes 131088 | tf_op jit(solution)/shard_map/psum | solution.py:166
  309.9 1.7 copy.179
  311.6 57.2 %all-gather.16.cloned.1.call-done = f32[4096,128]{0,1:T(8,128)} async-done(((f32[128,128]{0,1:T(8,128)}), f32[4096,128]{0,1:T(8,128)}) %all-gather.16.cloned.1.call-update) | async-done | bytes 2097168 | tf_op jit(solution)/shard_map/all_gather | solution.py:167
  368.8 2.0 copy.215
  371.8 6.4 %reduce-scatter.8.cloned.1.call-done = f32[256,128]{1,0:T(8,128)} async-done(((f32[512,128]{1,0:T(8,128)}), f32[256,128]{1,0:T(8,128)}) %reduce-scatter.8.cloned.1.call-update) | async-done | bytes 131088 | tf_op jit(solution)/shard_map/reduce_scatter | solution.py:164
  378.1 11.7 %reduce-scatter.6.cloned.1.call-done = f32[256,128]{1,0:T(8,128)} async-done(((f32[512,128]{1,0:T(8,128)}), f32[256,128]{1,0:T(8,128)}) %reduce-scatter.6.cloned.1.call-update) | async-done | bytes 131088 | tf_op jit(solution)/shard_map/reduce_scatter | solution.py:163
  (203 shorter events, 42.8 us)
Async XLA Ops:
  7.2 1.9 copy-start
  7.2 62.0 %all-gather.12.cloned.1.call-start = ((), (), s32[]{:S(2)}) async-start(), calls=%async_computation.7 | async-start | bytes 1114112 | tf_op jit(solution)/shard_map/all_gather | solution.py:9
  8.7 1.7 copy-start.32
  8.7 1.7 copy-start.33
  10.3 3.9 copy-start.34
  10.3 138.3 %reduce-scatter.4.cloned.1.call-start = ((), (), s32[]{:S(2)}) async-start(), calls=%async_computation.3 | async-start | bytes 196608 | tf_op jit(solution)/shard_map/reduce_scatter | solution.py:153
  10.5 47.5 %copy-start.10 = (f32[512,256]{1,0:T(8,128)S(1)}, f32[512,256]{1,0:T(8,128)}, u32[]{:S(2)}) copy-start(f32[512,256]{1,0:T(8,128)} %param.12) | copy-start | bytes 1572868
  14.0 46.7 %copy-start.12 = (f32[4,256]{0,1:T(8,128)}, f32[4,256]{0,1:T(8,128)S(1)}, u32[]{:S(2)}) copy-start(f32[4,256]{0,1:T(8,128)S(1)} %reduce_sum.213) | copy-start | bytes 12292
  60.9 23.6 %copy-start.13 = (f32[4,256]{0,1:T(8,128)S(1)}, f32[4,256]{0,1:T(8,128)}, u32[]{:S(2)}) copy-start(f32[4,256]{0,1:T(8,128)} %copy-done.12) | copy-start | bytes 12292
  88.9 2.2 copy-start.31
  88.9 2.2 copy-start.1
  88.9 2.2 copy-start.20
  90.0 2.7 copy-start.30
  90.0 2.7 copy-start.16
  91.1 3.1 copy-start.26
  92.2 6.8 %copy-start.14 = (f32[4,128,128]{1,2,0:T(8,128)}, f32[4,128,128]{1,2,0:T(8,128)S(1)}, u32[]{:S(2)}) copy-start(f32[4,128,128]{1,2,0:T(8,128)S(1)} %fusion.10) | copy-start | bytes 786436
  92.7 3.2 copy-start.27
  94.1 5.4 %copy-start.2 = (f32[4,128,128]{1,2,0:T(8,128)S(1)}, f32[4,128,128]{1,2,0:T(8,128)}, u32[]{:S(2)}) copy-start(f32[4,128,128]{1,2,0:T(8,128)} %copy.155) | copy-start | bytes 786436
  98.9 2.2 copy-start.15
  99.6 2.2 copy-start.17
  99.6 2.2 copy-start.28
  101.1 2.2 copy-start.23
  102.4 42.6 %copy-start.22 = (f32[512,128]{1,0:T(8,128)S(1)}, f32[512,128]{1,0:T(8,128)}, u32[]{:S(2)}) copy-start(f32[512,128]{1,0:T(8,128)} %get-tuple-element.336) | copy-start | bytes 786436
  104.6 95.2 %all-gather.14.cloned.1.call-start = ((), (), s32[]{:S(2)}) async-start(), calls=%async_computation.8 | async-start | bytes 1114112 | tf_op jit(solution)/shard_map/all_gather | solution.py:9
  148.7 161.3 %all-reduce.3.cloned.1.call-start = ((), (), s32[]{:S(2)}) async-start(), calls=%async_computation.6 | async-start | bytes 262144 | tf_op jit(solution)/shard_map/psum | solution.py:166
  156.5 2.3 copy-start.11
  156.5 2.7 copy-start.8
  156.5 2.7 copy-start.9
  158.8 0.7 copy-start.4
  159.4 42.8 %copy-start.29 = (f32[128]{0:T(128)S(1)}, f32[128]{0:T(128)}, u32[]{:S(2)}) copy-start(f32[128]{0:T(128)} %custom-call.3) | copy-start | bytes 1540
  159.5 42.6 %copy-start.6 = (f32[512,128]{0,1:T(8,128)}, f32[512,128]{0,1:T(8,128)S(1)}, u32[]{:S(2)}) copy-start(f32[512,128]{0,1:T(8,128)S(1)} %multiply_subtract_fusion.2) | copy-start | bytes 786436
  160.6 208.2 %all-gather.16.cloned.1.call-start = ((), (), s32[]{:S(2)}) async-start(), calls=%async_computation.9 | async-start | bytes 2162688 | tf_op jit(solution)/shard_map/all_gather | solution.py:167
  202.1 14.3 %copy-start.19 = (f32[512,128]{1,0:T(8,128)S(1)}, f32[512,128]{1,0:T(8,128)}, u32[]{:S(2)}) copy-start(f32[512,128]{1,0:T(8,128)} %param.13) | copy-start | bytes 786436
  215.8 1.7 copy-start.18
  216.3 4.0 copy-start.3
  216.5 3.8 copy-start.21
  217.5 160.6 %reduce-scatter.8.cloned.1.call-start = ((), (), s32[]{:S(2)}) async-start(), calls=%async_computation.5 | async-start | bytes 393216 | tf_op jit(solution)/shard_map/reduce_scatter | solution.py:164
  219.2 3.2 copy-start.5
  219.2 3.2 copy-start.24
  219.2 3.6 copy-start.25
  220.3 3.9 copy-start.7
  222.3 167.5 %reduce-scatter.6.cloned.1.call-start = ((), (), s32[]{:S(2)}) async-start(), calls=%async_computation.4 | async-start | bytes 393216 | tf_op jit(solution)/shard_map/reduce_scatter | solution.py:163
Sparse Core Ops, SparseCore 0:
  11.3 57.8 all-gather.11
  104.7 6.4 reduce-scatter.3
  148.8 50.9 all-gather.13
  205.6 104.2 all-reduce.2
  313.2 55.5 all-gather.15
  371.5 6.5 reduce-scatter.7
  380.9 8.8 reduce-scatter.5
